TPU v7x, 512 devices: a whole 4x4x16 slice. The times are simulated.
512 devices in a mesh: lat: 64 (over z, y), wid: 2 (over core), tok: 4 (over x).
Axes of the slice: x: 4, y: 4, z: 16, core: 2. Of those that a mesh axis runs over, the one named last changes fastest.
Arguments:
- resid: bfloat16 [512, 4096], P('tok', 'wid'), may hold values from -6 to 6
- dictionary: bfloat16 [32768, 4096], P('lat', 'wid'), may hold values from -0.1875 to 0.1875
- enc_bias: float32 [32768], P('lat'), may hold values from -3 to 3
- dec_bias: float32 [4096], P('wid'), may hold values from -3 to 3
- active_blocks: int32 [512, 8], P('tok'), may hold values from 0 to 255, all different within a row
- level_bounds: int32 [4], replicated, may hold values from 1 to 256, as said below
Outputs:
- level_losses: float32 [4], replicated
- dict_grad: bfloat16 [4096, 32768], P(('wid', 'tok'), 'lat')
Inputs may be any that keep to these rules, and one draw needn't show every extreme that they name: `active_blocks`: each row names 8 different blocks. `level_bounds`: strictly increasing; the last equals 256.
All inputs are finite; a program needn't handle non-finite values.
Results may differ from a plain program's by a relative error of at most 0.006.
Values sent between devices are 32-bit elements; how exact they have to be, the bound alone decides.
A program may use at most 192 MiB of HBM per device.

v0:
```python
import jax
import jax.numpy as jnp
from jax import lax
from jax.sharding import PartitionSpec as P

LEVELS = 4


def entering(part, axis, combine, identity):
    place = lax.axis_index(axis)
    gathered = lax.all_gather(part, axis)
    state = jnp.zeros_like(part) + jnp.asarray(identity, part.dtype)

    def one(turn, state):
        return combine(state, lax.dynamic_index_in_dim(gathered, turn, 0, False))

    return lax.fori_loop(0, place, one, state)


def broadcast(array, axis, root):
    mine = lax.axis_index(axis) == root
    return lax.psum(jnp.where(mine, array, jnp.zeros_like(array)), axis)


def gelu_tanh(value):
    return jax.nn.gelu(value, approximate=True)


def add_pair(earlier, later):
    return earlier + later


def body(resid, dictionary, enc_bias, dec_bias, active_blocks, level_bounds):
    row_count, half_width = resid.shape
    lat_count = dictionary.shape[0]
    blocks_here = lat_count // 128
    lat_position = lax.axis_index("lat")
    first_block = lat_position * blocks_here
    local_ids = first_block + jnp.arange(blocks_here, dtype=jnp.int32)
    resid_full = resid.astype(jnp.float32)
    dict_blocks = dictionary.reshape(blocks_here, 128, half_width)
    partial_pre = lax.dot_general(
        resid, dictionary, (((1,), (1,)), ((), ())), preferred_element_type=jnp.float32
    )
    pre = lax.psum(partial_pre, "wid") + enc_bias[None, :]
    hits = jnp.any(active_blocks[:, :, None] == local_ids[None, None, :], axis=1).astype(
        jnp.float32
    )
    act = (gelu_tanh(pre).reshape(row_count, blocks_here, 128) * hits[:, :, None]).astype(
        jnp.bfloat16
    )
    act_flat = act.reshape(row_count, lat_count)
    latent_block = jnp.arange(lat_count, dtype=jnp.int32) // 128
    owners = []
    keeps = []
    for level in range(LEVELS):
        bound = level_bounds[level]
        owners.append((bound - 1) // blocks_here)
        inside = jnp.clip(bound - 1 - first_block, 0, blocks_here - 1)
        keeps.append(latent_block <= inside)
    keeps.append(latent_block >= 0)
    keep_rows = jnp.stack(keeps)
    act_stack = jnp.where(keep_rows[:, None, :], act_flat[None], jnp.zeros((), jnp.bfloat16))
    partials = jnp.dot(
        act_stack.reshape((LEVELS + 1) * row_count, lat_count),
        dictionary,
        preferred_element_type=jnp.float32,
    )
    partials = partials.reshape(LEVELS + 1, row_count, half_width)
    zeros_field = jnp.zeros((row_count, half_width), jnp.float32)
    earlier = entering(partials[LEVELS], "lat", add_pair, zeros_field)
    own_errors = []
    squares = []
    for level in range(LEVELS):
        mine = owners[level] == lat_position
        error = dec_bias[None, :] + earlier + partials[level] - resid_full
        own_errors.append(jnp.where(mine, error, 0.0))
        squares.append(jnp.where(mine, jnp.sum(error * error), 0.0))
    include = (level_bounds[:, None] > local_ids[None, :]).astype(jnp.float32)
    err_sum = None
    for level in range(LEVELS):
        level_err = broadcast(own_errors[level], "lat", owners[level])
        term = include[level][:, None, None] * level_err[None]
        err_sum = term if err_sum is None else err_sum + term
    err_half = err_sum.astype(jnp.bfloat16)
    partial_adjoint = jnp.einsum(
        "ktd,kcd->tkc", err_half, dict_blocks, preferred_element_type=jnp.float32
    )
    g_act = lax.psum(partial_adjoint.reshape(row_count, lat_count), "wid")
    mask_full = jnp.broadcast_to(hits[:, :, None], (row_count, blocks_here, 128)).reshape(
        row_count, lat_count
    )
    _, pull = jax.vjp(gelu_tanh, pre)
    g_pre = pull(g_act * mask_full)[0].astype(jnp.bfloat16)
    decode_term = jnp.einsum("ktd,tkc->dkc", err_half, act, preferred_element_type=jnp.float32)
    encode_term = lax.dot_general(
        resid, g_pre, (((0,), (0,)), ((), ())), preferred_element_type=jnp.float32
    )
    grad_share = lax.psum_scatter(
        decode_term.reshape(half_width // lax.axis_size("tok") * lax.axis_size("tok"), lat_count)
        + encode_term,
        "tok",
        scatter_dimension=0,
        tiled=True,
    )
    total_sq = lax.psum(jnp.stack(squares), ("lat", "wid", "tok"))
    level_losses = total_sq / (row_count * lax.axis_size("tok") * half_width * lax.axis_size("wid"))
    return (level_losses, grad_share.astype(jnp.bfloat16))


def solution(mesh):
    return jax.shard_map(
        body,
        mesh=mesh,
        in_specs=(P("tok", "wid"), P("lat", "wid"), P("lat"), P("wid"), P("tok", None), P()),
        out_specs=(P(), P(("wid", "tok"), "lat")),
        check_vma=False,
    )
```

profile of v0, /device:TPU:1, one launch (start us, length us, event | category | flops | bytes accessed | tf_op | source)
XLA Modules:
  0.0 1121.9 jit_solution(13684418029557174763)
XLA Ops:
  7.2 0.0 copy-start
  7.2 0.0 all-reduce.5.cloned.1.call-start
  7.2 1.5 copy-done
  8.8 2.6 fusion.25
  11.3 0.0 all-reduce.5.cloned.1.call-update
  11.4 0.0 all-gather.3.cloned.1.call-start
  11.4 1.5 fusion.23
  12.9 0.8 compare_reduce_fusion
  16.2 0.1 copy.17
  16.4 41.2 %all-reduce.5.cloned.1.call-done = f32[128,512]{1,0:T(8,128)} async-done(((f32[128,512]{1,0:T(8,128)}), f32[128,512]{1,0:T(8,128)}) %all-reduce.5.cloned.1.call-update) | async-done | bytes 262160 | tf_op jit(solution)/shard_map/psum | solution.py:45
  57.6 1.8 multiply_convert_fusion.1
  59.4 1.6 fusion.26
  61.0 0.0 copy-start.1
  61.0 2.3 copy-done.1
  63.3 1.1 slice.60
  64.4 0.0 all-gather.3.cloned.1.call-update
  64.4 0.0 all-reduce.9.cloned.1.call-start
  64.6 512.8 %all-gather.3.cloned.1.call-done = f32[8192,2048]{1,0:T(8,128)} async-done(((f32[128,2048]{1,0:T(8,128)}), f32[8192,2048]{1,0:T(8,128)}) %all-gather.3.cloned.1.call-update) | async-done | bytes 67108880 | tf_op jit(solution)/shard_map/all_gather | solution.py:11
  577.4 0.1 broadcast.226
  577.5 0.0 copy-start.6
  577.6 0.7 copy-done.6
  578.2 5.8 select_select_fusion.3
  584.0 0.0 copy-start.5
  584.0 0.0 copy-start.3
  584.0 0.0 all-reduce.9.cloned.1.call-update
  584.0 0.0 all-reduce.7.cloned.1.call-start
  584.1 0.6 copy-done.5
  584.7 0.1 compare_convert_fusion
  584.7 0.2 copy-done.3
  585.0 0.1 copy.18
  585.1 365.0 %all-reduce.9.cloned.1.call-done = (f32[128,2048]{1,0:T(8,128)}, f32[128,2048]{1,0:T(8,128)}, f32[128,2048]{1,0:T(8,128)}, f32[128,2048]{1,0:T(8,128)}) async-done(((f32[128,2048]{1,0:T(8,128)}, f32[128,2048]{1,0:T(8,128)}, f32[128,2048]{1,0:T(8,128)}, f32[128,2048]{1,0:T(8,128)}), (f32[128,2048]{1,0:T(8,128)}, f32[128,2048]{1,0:T(8,128)}, f32[128,2048]{1,0:T(8,128)}, ...) | async-done | bytes 4194320 | tf_op jit(solution)/shard_map/psum | solution.py:22
  950.1 3.5 fusion.24
  953.6 0.8 copy.19
  954.4 0.0 all-reduce.7.cloned.1.call-update
  954.5 0.0 reduce-scatter.2.cloned.1.call-start
  954.5 0.0 copy-start.2
  954.5 0.0 copy-start.4
  954.5 0.0 copy-start.7
  954.6 5.7 fusion.7
  960.2 39.1 %all-reduce.7.cloned.1.call-done = f32[128,512]{1,0:T(8,128)} async-done(((f32[128,512]{1,0:T(8,128)}), f32[128,512]{1,0:T(8,128)}) %all-reduce.7.cloned.1.call-update) | async-done | bytes 262160 | tf_op jit(solution)/shard_map/psum | solution.py:89
  999.3 0.0 copy-done.2
  999.3 0.0 copy-done.4
  999.3 0.0 copy-done.7
  999.3 5.1 bitcast_add_fusion.1
  1004.4 0.0 reduce-scatter.2.cloned.1.call-update
  1007.1 0.1 pad_maximum_fusion
  1007.1 105.4 %psum.50 = f32[4]{0:T(128)S(1)} all-reduce(f32[4]{0:T(128)S(1)} %pad_maximum_fusion), channel_id=1, replica_groups=mesh['lat'=64,'wid'=2,'tok'=4] {'lat','wid','tok'}, use_global_device_ids=true, to_apply=%region_8.9 | all-reduce | flops 4 | bytes 32 | tf_op jit(solution)/shard_map/psum | solution.py:106
  1112.6 0.5 broadcast_multiply_fusion
  1113.1 0.0 reduce-scatter.2.cloned.1.call-done
  1113.1 1.3 convert_element_type.36
  1114.4 1.0 copy.16
  (10 shorter events, 0.2 us)
Async XLA Ops:
  7.2 1.6 copy-start
  7.2 50.4 %all-reduce.5.cloned.1.call-start = ((), (), s32[]{:S(2)}) async-start(), calls=%async_computation.1 | async-start | bytes 524288 | tf_op jit(solution)/shard_map/psum | solution.py:45
  11.4 566.1 %all-gather.3.cloned.1.call-start = ((), (), s32[]{:S(2)}) async-start(), calls=%async_computation.4 | async-start | bytes 68157440 | tf_op jit(solution)/shard_map/all_gather | solution.py:11
  61.0 2.3 copy-start.1
  64.4 885.7 %all-reduce.9.cloned.1.call-start = ((), (), s32[]{:S(2)}) async-start(), calls=%async_computation.5 | async-start | bytes 8388608 | tf_op jit(solution)/shard_map/psum | solution.py:22
  577.5 0.7 copy-start.6
  584.0 0.7 copy-start.5
  584.0 1.0 copy-start.3
  584.0 415.3 %all-reduce.7.cloned.1.call-start = ((), (), s32[]{:S(2)}) async-start(), calls=%async_computation.2 | async-start | bytes 524288 | tf_op jit(solution)/shard_map/psum | solution.py:89
  954.5 158.6 %reduce-scatter.2.cloned.1.call-start = ((), (), s32[]{:S(2)}) async-start(), calls=%async_computation.3 | async-start | bytes 5242880 | tf_op jit(solution)/shard_map/reduce_scatter | solution.py:99
  954.5 44.8 %copy-start.2 = (bf16[128,2048]{1,0:T(8,128)(2,1)S(1)}, bf16[128,2048]{1,0:T(8,128)(2,1)}, u32[]{:S(2)}) copy-start(bf16[128,2048]{1,0:T(8,128)(2,1)} %param.8) | copy-start | bytes 1572868
  954.5 44.8 %copy-start.4 = (f32[128,512]{1,0:T(8,128)S(1)}, f32[128,512]{1,0:T(8,128)}, u32[]{:S(2)}) copy-start(f32[128,512]{1,0:T(8,128)} %all-reduce.5.cloned.1.call-done) | copy-start | bytes 786436
  954.5 44.8 %copy-start.7 = (f32[512]{0:T(512)S(1)}, f32[512]{0:T(512)}, u32[]{:S(2)}) copy-start(f32[512]{0:T(512)} %param.10) | copy-start | bytes 6148
Sparse Core Ops, SparseCore 0:
  11.5 46.0 all-reduce.4
  64.6 512.8 all-gather.2
  584.2 365.8 all-reduce.8
  954.6 44.6 all-reduce.6
  1004.6 54.7 reduce-scatter.1
where the time goes:
time: 1120 us
  waiting for transfers between devices  958 us (86%)
  blocking collectives  105 us (9%)
  between operations  19.2 us (2%)
  matrix products  18.4 us (2%)
    all_gather x1, waiting for transfers between devices, entering(): gathered = lax.all_gather(part, axis)  513 us
    psum x1, waiting for transfers between devices, broadcast(): return lax.psum(jnp.where(mine, array, jnp.zeros_like(array)), axis)  365 us
    psum x1, blocking collectives, body(): total_sq = lax.psum(jnp.stack(squares), ('lat', 'wid', 'tok'))  105 us
    psum x1, waiting for transfers between devices, body(): pre = lax.psum(partial_pre, 'wid') + enc_bias[None, :]  41.2 us
    psum x1, waiting for transfers between devices, body(): g_act = lax.psum(partial_adjoint.reshape(row_count, lat_count), 'wid')  39.1 us
  transfers between devices with their start and end apart: 5, of which 4 were waited for; matrix products, arithmetic and copies ran while one was open for 1% of the time, Pallas kernels for 0%

commit v1 on v0

--- a/solution.py
+++ b/solution.py
@@ -103,7 +103,7 @@
         scatter_dimension=0,
         tiled=True,
     )
-    total_sq = lax.psum(jnp.stack(squares), ("lat", "wid", "tok"))
+    total_sq = jnp.sum(lax.all_gather(jnp.stack(squares), ("lat", "wid", "tok")), axis=0)
     level_losses = total_sq / (row_count * lax.axis_size("tok") * half_width * lax.axis_size("wid"))
     return (level_losses, grad_share.astype(jnp.bfloat16))
 

time: 1120 us -> 1130 us (level)
    unnamed x0 -> x1, blocking collectives: none -> 105 us
    psum x1 -> x0, blocking collectives: 105 us -> none  [body(): total_sq = lax.psum(jnp.stack(squares), ('lat', 'wid', 'tok'))]
where the time goes in v1:
time: 1130 us; the launch traced here: 1120 us
  waiting for transfers between devices  958 us (85%)
  blocking collectives  105 us (9%)
  between operations  19 us (2%)
  matrix products  18.4 us (2%)
    all_gather x1, waiting for transfers between devices, entering(): gathered = lax.all_gather(part, axis)  513 us
    psum x1, waiting for transfers between devices, broadcast(): return lax.psum(jnp.where(mine, array, jnp.zeros_like(array)), axis)  365 us
    unnamed x1, blocking collectives  105 us
    psum x1, waiting for transfers between devices, body(): pre = lax.psum(partial_pre, 'wid') + enc_bias[None, :]  41.1 us
    psum x1, waiting for transfers between devices, body(): g_act = lax.psum(partial_adjoint.reshape(row_count, lat_count), 'wid')  39.1 us
  transfers between devices with their start and end apart: 5, of which 4 were waited for; matrix products, arithmetic and copies ran while one was open for 1% of the time, Pallas kernels for 0%

profile of v1, /device:TPU:1, one launch (start us, length us, event | category | flops | bytes accessed | tf_op | source)
XLA Modules:
  0.0 1122.6 jit_solution(13241242316353111017)
XLA Ops:
  7.2 0.0 copy-start
  7.2 0.0 all-reduce.6.cloned.1.call-start
  7.2 1.5 copy-done
  8.8 2.6 fusion.25
  11.3 0.0 all-reduce.6.cloned.1.call-update
  11.4 0.0 all-gather.4.cloned.1.call-start
  11.4 1.5 fusion.23
  12.9 0.8 compare_reduce_fusion
  16.3 0.1 copy.22
  16.5 41.1 %all-reduce.6.cloned.1.call-done = f32[128,512]{1,0:T(8,128)} async-done(((f32[128,512]{1,0:T(8,128)}), f32[128,512]{1,0:T(8,128)}) %all-reduce.6.cloned.1.call-update) | async-done | bytes 262160 | tf_op jit(solution)/shard_map/psum | solution.py:45
  57.6 1.8 multiply_convert_fusion.1
  59.4 1.6 fusion.26
  61.0 0.0 copy-start.1
  61.0 2.3 copy-done.1
  63.3 1.1 slice.60
  64.4 0.0 all-gather.4.cloned.1.call-update
  64.5 0.0 all-reduce.10.cloned.1.call-start
  64.6 512.8 %all-gather.4.cloned.1.call-done = f32[8192,2048]{1,0:T(8,128)} async-done(((f32[128,2048]{1,0:T(8,128)}), f32[8192,2048]{1,0:T(8,128)}) %all-gather.4.cloned.1.call-update) | async-done | bytes 67108880 | tf_op jit(solution)/shard_map/all_gather | solution.py:11
  577.5 0.1 broadcast.226
  577.6 0.0 copy-start.6
  577.6 0.7 copy-done.6
  578.3 5.7 select_select_fusion.3
  584.0 0.0 copy-start.5
  584.0 0.0 copy-start.3
  584.0 0.0 all-reduce.10.cloned.1.call-update
  584.0 0.0 all-reduce.8.cloned.1.call-start
  584.1 0.6 copy-done.5
  584.6 0.1 compare_convert_fusion
  584.7 0.2 copy-done.3
  585.0 0.1 copy.23
  585.1 365.3 %all-reduce.10.cloned.1.call-done = (f32[128,2048]{1,0:T(8,128)}, f32[128,2048]{1,0:T(8,128)}, f32[128,2048]{1,0:T(8,128)}, f32[128,2048]{1,0:T(8,128)}) async-done(((f32[128,2048]{1,0:T(8,128)}, f32[128,2048]{1,0:T(8,128)}, f32[128,2048]{1,0:T(8,128)}, f32[128,2048]{1,0:T(8,128)}), (f32[128,2048]{1,0:T(8,128)}, f32[128,2048]{1,0:T(8,128)}, f32[128,2048]{1,0:T(8,128)}, ...) | async-done | bytes 4194320 | tf_op jit(solution)/shard_map/psum | solution.py:22
  950.4 3.5 fusion.24
  953.9 0.8 copy.24
  954.7 0.0 all-reduce.8.cloned.1.call-update
  954.8 0.0 reduce-scatter.2.cloned.1.call-start
  954.8 0.0 copy-start.2
  954.8 0.0 copy-start.4
  954.8 0.0 copy-start.7
  954.9 5.7 fusion.7
  960.5 39.1 %all-reduce.8.cloned.1.call-done = f32[128,512]{1,0:T(8,128)} async-done(((f32[128,512]{1,0:T(8,128)}), f32[128,512]{1,0:T(8,128)}) %all-reduce.8.cloned.1.call-update) | async-done | bytes 262160 | tf_op jit(solution)/shard_map/psum | solution.py:89
  999.6 0.0 copy-done.2
  999.6 0.0 copy-done.4
  999.6 0.0 copy-done.7
  999.6 5.1 bitcast_add_fusion.1
  1004.7 0.0 reduce-scatter.2.cloned.1.call-update
  1007.2 0.2 maximum_dynamic-update-slice_fusion
  1007.4 105.5 %all-reduce = f32[2048]{0:T(1024)S(1)} all-reduce(f32[2048]{0:T(1024)S(1)} %maximum_dynamic-update-slice_fusion), channel_id=3, replica_groups=mesh['lat'=64,'wid'=2,'tok'=4] {'lat','wid','tok'}, use_global_device_ids=true, to_apply=%add | all-reduce | flops 2048 | bytes 16384
  1112.9 0.3 reshape.130
  1113.1 0.1 reduce_sum.49
  1113.2 0.5 broadcast_multiply_fusion
  1113.7 0.0 reduce-scatter.2.cloned.1.call-done
  1113.7 1.3 convert_element_type.36
  1115.0 1.0 copy.21
  (11 shorter events, 0.2 us)
Async XLA Ops:
  7.2 1.6 copy-start
  7.2 50.4 %all-reduce.6.cloned.1.call-start = ((), (), s32[]{:S(2)}) async-start(), calls=%async_computation.1 | async-start | bytes 524288 | tf_op jit(solution)/shard_map/psum | solution.py:45
  11.4 566.1 %all-gather.4.cloned.1.call-start = ((), (), s32[]{:S(2)}) async-start(), calls=%async_computation.4 | async-start | bytes 68157440 | tf_op jit(solution)/shard_map/all_gather | solution.py:11
  61.0 2.3 copy-start.1
  64.5 885.9 %all-reduce.10.cloned.1.call-start = ((), (), s32[]{:S(2)}) async-start(), calls=%async_computation.5 | async-start | bytes 8388608 | tf_op jit(solution)/shard_map/psum | solution.py:22
  577.6 0.7 copy-start.6
  584.0 0.7 copy-start.5
  584.0 1.0 copy-start.3
  584.0 415.6 %all-reduce.8.cloned.1.call-start = ((), (), s32[]{:S(2)}) async-start(), calls=%async_computation.2 | async-start | bytes 524288 | tf_op jit(solution)/shard_map/psum | solution.py:89
  954.8 159.0 %reduce-scatter.2.cloned.1.call-start = ((), (), s32[]{:S(2)}) async-start(), calls=%async_computation.3 | async-start | bytes 5242880 | tf_op jit(solution)/shard_map/reduce_scatter | solution.py:99
  954.8 44.8 %copy-start.2 = (bf16[128,2048]{1,0:T(8,128)(2,1)S(1)}, bf16[128,2048]{1,0:T(8,128)(2,1)}, u32[]{:S(2)}) copy-start(bf16[128,2048]{1,0:T(8,128)(2,1)} %param.8) | copy-start | bytes 1572868
  954.8 44.8 %copy-start.4 = (f32[128,512]{1,0:T(8,128)S(1)}, f32[128,512]{1,0:T(8,128)}, u32[]{:S(2)}) copy-start(f32[128,512]{1,0:T(8,128)} %all-reduce.6.cloned.1.call-done) | copy-start | bytes 786436
  954.8 44.8 %copy-start.7 = (f32[512]{0:T(512)S(1)}, f32[512]{0:T(512)}, u32[]{:S(2)}) copy-start(f32[512]{0:T(512)} %param.10) | copy-start | bytes 6148
Sparse Core Ops, SparseCore 0:
  11.5 46.0 all-reduce.5
  64.6 512.8 all-gather.3
  584.1 366.2 all-reduce.9
  954.9 44.6 all-reduce.7
  1004.9 54.7 reduce-scatter.1
